TPU v7x, 256 devices: a whole 4x4x8 slice. The times are simulated.
256 devices in a mesh: section: 8 (over x, core), fsdp: 8 (over z), seq: 4 (over y).
Axes of the slice: x: 4, y: 4, z: 8, core: 2. Of those that a mesh axis runs over, the one named last changes fastest.
Arguments:
- acts: bfloat16 [8, 8, 512, 1536], P('section', 'fsdp', 'seq')
- grad_out: bfloat16 [8, 512, 1536], P('fsdp', 'seq'), may hold values from -6 to 6
- gain: float32 [8, 1536], P('section'), may hold values from 0.5 to 2
- gate: float32 [8, 1536], P('section'), may hold values from 0.5 to 2
- w_query: bfloat16 [8, 1536, 1536], P('section', ('fsdp', 'seq'))
- kept: int32 [8, 8], P('fsdp'), may hold values from 0 to 1, as said below
- links: int32 [8, 4], P('fsdp', 'seq'), may hold values from 0 to 1, as said below
Outputs:
- grad_acts: bfloat16 [8, 8, 512, 1536], P('section', 'fsdp', 'seq')
- grad_wq: bfloat16 [8, 1536, 1536], P('section', ('fsdp', 'seq'))
Inputs may be any that keep to these rules, and one draw needn't show every extreme that they name: `kept`: clip 0 runs every layer; the other entries vary. `links`: in clip 0 every tile after the first attends the tile before it; the other entries vary.
All inputs are finite; a program needn't handle non-finite values.
Results may differ from a plain program's by a relative error of at most 0.025.
The roundings to bfloat16 on the way count: a program that leaves them out, or rounds other values in their place, can miss the bound.
Values may be sent and summed in bfloat16 or wider, within the bound.
A program may use at most 64 MiB of HBM per device.

v0:
```python
import jax
import jax.numpy as jnp
from jax import lax
from jax.sharding import PartitionSpec as P

HDIM = 128


norm_eps = 1e-06
head_pair = 2


def from_behind(value, axis, steps):
    count = lax.axis_size(axis)
    initial, last = (max(0, -steps), min(count, count - steps))
    return lax.ppermute(value, axis, [(source, source + steps) for source in range(initial, last)])


def split_heads(token_rows):
    tokens_here = token_rows.shape[0]
    return token_rows.reshape(
        tokens_here, token_rows.shape[1] // (head_pair * HDIM), head_pair, HDIM
    ).transpose(1, 2, 0, 3)


def merge_heads(blocks):
    return blocks.transpose(2, 0, 1, 3).reshape(blocks.shape[2], -1)


def head_grads(query_heads, key_heads, grad_heads, key_valid, score_scale):

    def per_group(operands):
        query_part, key_part, grad_part = operands
        scores = (
            jnp.einsum("gid,gjd->gij", query_part, key_part, preferred_element_type=jnp.float32)
            * score_scale
        )
        scores = jnp.where(key_valid[None, None, :], scores, -1e30)
        row_max = jnp.max(scores, axis=-1, keepdims=True)
        exp_scores = jnp.exp(scores - row_max)
        prob_rows = exp_scores / jnp.sum(exp_scores, axis=-1, keepdims=True)
        probs_low = prob_rows.astype(jnp.bfloat16)
        prob_grad = jnp.einsum(
            "gid,gjd->gij", grad_part, key_part, preferred_element_type=jnp.float32
        )
        row_delta = jnp.sum(prob_rows * prob_grad, axis=-1, keepdims=True)
        score_grad = (prob_rows * (prob_grad - row_delta) * score_scale).astype(jnp.bfloat16)
        query_grad = jnp.einsum(
            "gij,gjd->gid", score_grad, key_part, preferred_element_type=jnp.float32
        ).astype(jnp.bfloat16)
        key_grad = jnp.einsum(
            "gij,gid->gjd", score_grad, query_part, preferred_element_type=jnp.float32
        )
        key_grad = key_grad + jnp.einsum(
            "gij,gid->gjd", probs_low, grad_part, preferred_element_type=jnp.float32
        )
        return (query_grad, key_grad)

    return lax.map(per_group, (query_heads, key_heads, grad_heads))


def per_device(acts, grad_out, gain, gate, w_query, kept, links):
    sections = lax.axis_size("section")
    section_idx = lax.axis_index("section")
    seq_idx = lax.axis_index("seq")
    score_scale = HDIM ** (-0.5)
    gain_row = gain[0]
    gate_row = gate[0]
    x_rows = acts[0, 0].astype(jnp.float32)
    inv_rms = lax.rsqrt(jnp.mean(x_rows * x_rows, axis=-1, keepdims=True) + norm_eps)
    normed = (x_rows * inv_rms * gain_row).astype(jnp.bfloat16)
    left_normed = from_behind(normed, "seq", 1)
    weights = lax.all_gather(w_query, ("fsdp", "seq"), axis=1, tiled=True)[0]
    tile_rows = normed.shape[0]
    key_heads = split_heads(jnp.concatenate([left_normed, normed], axis=0))
    linked = links[0, 0] * (seq_idx > 0).astype(jnp.int32) > 0
    key_valid = jnp.concatenate(
        [jnp.broadcast_to(linked, (tile_rows,)), jnp.ones((tile_rows,), dtype=jnp.bool_)]
    )
    keep_flag = lax.dynamic_index_in_dim(kept[0], section_idx, keepdims=False) > 0

    def layer_work(incoming):
        query_rows = jnp.dot(normed, weights, preferred_element_type=jnp.float32).astype(
            jnp.bfloat16
        )
        out_grad = (gate_row * incoming.astype(jnp.float32)).astype(jnp.bfloat16)
        query_grad, key_grad = head_grads(
            split_heads(query_rows), key_heads, split_heads(out_grad), key_valid, score_scale
        )
        query_grad = merge_heads(query_grad)
        key_grad = merge_heads(key_grad)
        own_grad = lax.dot_general(
            query_grad, weights, (((1,), (1,)), ((), ())), preferred_element_type=jnp.float32
        )
        own_grad = own_grad + key_grad[tile_rows:]
        return (query_grad, own_grad, key_grad[:tile_rows].astype(jnp.bfloat16))

    def layer_skip(incoming):
        return (
            jnp.zeros_like(normed),
            jnp.zeros(normed.shape, jnp.float32),
            jnp.zeros_like(normed),
        )

    incoming = jnp.where(section_idx == sections - 1, grad_out[0], jnp.zeros_like(grad_out[0]))
    result = jnp.zeros_like(grad_out[0])
    kept_grad = jnp.zeros_like(normed)
    for tick_index in range(sections):
        active = section_idx == sections - 1 - tick_index
        runs_now = jnp.logical_and(active, keep_flag)
        query_grad, own_grad, leftward = lax.cond(runs_now, layer_work, layer_skip, incoming)
        returned = from_behind(leftward, "seq", -1)
        scaled_grad = (own_grad + returned.astype(jnp.float32)) * gain_row
        mean_term = jnp.mean(x_rows * scaled_grad, axis=-1, keepdims=True)
        change = inv_rms * (scaled_grad - x_rows * inv_rms * inv_rms * mean_term)
        updated = jnp.where(
            runs_now, (incoming.astype(jnp.float32) + change).astype(jnp.bfloat16), incoming
        )
        result = jnp.where(active, updated, result)
        kept_grad = jnp.where(active, query_grad, kept_grad)
        if tick_index + 1 < sections:
            incoming = from_behind(updated, "section", -1)
    grad_rows = lax.psum_scatter(
        lax.dot_general(
            normed, kept_grad, (((0,), (0,)), ((), ())), preferred_element_type=jnp.float32
        ).astype(jnp.bfloat16),
        ("fsdp", "seq"),
        scatter_dimension=0,
        tiled=True,
    )
    return (result[None, None], grad_rows[None])


def solution(mesh):
    placed = (
        P("section", "fsdp", "seq", None),
        P("fsdp", "seq", None),
        P("section", None),
        P("section", None),
        P("section", ("fsdp", "seq"), None),
        P("fsdp", None),
        P("fsdp", "seq"),
    )
    return jax.shard_map(
        per_device,
        mesh=mesh,
        in_specs=placed,
        out_specs=(P("section", "fsdp", "seq", None), P("section", ("fsdp", "seq"), None)),
        check_vma=False,
    )
```

profile of v0, /device:TPU:32, one launch (start us, length us, event | category | flops | bytes accessed | tf_op | source)
XLA Modules:
  0.0 1069.5 jit_solution(1735687744858287852)
XLA Ops:
  11.0 3.5 collective-permute-start
  17.8 5.1 collective-permute-done
  23.2 72.7 %all-gather.2.cloned.1.call-done = bf16[1,1536,1536]{2,1,0:T(8,128)(2,1)} async-done(((bf16[1,48,1536]{2,1,0:T(8,128)(2,1)}), bf16[1,1536,1536]{2,1,0:T(8,128)(2,1)}) %all-gather.2.cloned.1.call-update) | async-done | bytes 4718608 | tf_op jit(solution)/shard_map/all_gather | solution.py:73
  98.3 8.6 collective-permute-done.1
  112.9 8.4 collective-permute-done.3
  125.1 5.3 collective-permute-done.4
  133.6 8.6 collective-permute-done.5
  145.6 8.9 collective-permute-done.6
  158.6 8.6 collective-permute-done.7
  170.6 7.7 collective-permute-done.8
  182.4 8.6 collective-permute-done.9
  194.4 7.5 collective-permute-done.10
  206.2 8.6 collective-permute-done.11
  218.2 6.2 collective-permute-done.12
  228.4 8.6 collective-permute-done.13
  240.4 314.3 %collective-permute-done.14 = bf16[128,1536]{1,0:T(8,128)(2,1)} collective-permute-done((bf16[128,1536]{1,0:T(8,128)(2,1)}, bf16[128,1536]{1,0:T(8,128)(2,1)}, u32[]{:S(2)}, u32[]{:S(2)}) %collective-permute-start.14) | collective-permute-done | bytes 393248 | tf_op jit(solution)/shard_map/ppermute | solution.py:16
  554.7 81.1 %conditional.15 = (bf16[128,1536]{1,0:T(8,128)(2,1)}, f32[128,1536]{1,0:T(8,128)S(1)}, bf16[128,1536]{1,0:T(8,128)(2,1)}) conditional(s32[]{:T(128)} %convert_element_type.317, () %tuple.118, (bf16[128,1536]{1,0:T(8,128)(2,1)S(1)}, bf16[1536,1536]{1,0:T(8,128)(2,1)}, f32[1,1536]{1,0:T(1,128)S(1)}, bf16[128,1536]{1,0:T(8,128)(2,1)}, ...), branch_computations={%region_57.58_spmd, %region_58.64_spmd} | conditional | flops 1311213312 | bytes 29916412 | solution.py:111
  557.2 3.1 convolution_convert_fusion.15
  560.9 60.6 %while.95 = (s32[]{:T(128)}, bf16[6,2,128,128]{3,2,1,0:T(8,128)(2,1)}, f32[6,2,256,128]{3,2,1,0:T(8,128)}, pred[256]{0:T(512)(128)(4,1)S(1)}, bf16[6,2,128,128]{...) while((s32[]{:T(128)}, ...), condition=%wide.region_63.63_spmd, body=%wide.region_59.62_spmd.sunk | while | flops 102270720 | bytes 4337761 | solution.py:59
  563.0 2.9 fusion.833
  565.9 2.8 fusion.832
  573.1 2.9 fusion.833
  576.0 2.8 fusion.832
  583.2 3.0 fusion.833
  593.3 3.0 fusion.833
  603.3 2.9 fusion.833
  606.3 2.8 fusion.832
  613.4 2.9 fusion.833
  630.2 4.2 convolution_add_fusion.15
  635.8 4.6 convolution_convert_fusion.16
  641.8 8.6 collective-permute-done.15
  653.3 409.1 %reduce-scatter.2.cloned.1.call-done = bf16[48,1536]{1,0:T(8,128)(2,1)} async-done(((bf16[1536,1536]{1,0:T(8,128)(2,1)}), bf16[48,1536]{1,0:T(8,128)(2,1)}) %reduce-scatter.2.cloned.1.call-update) | async-done | bytes 147472 | tf_op jit(solution)/shard_map/reduce_scatter | solution.py:123
  (179 shorter events, 110.1 us)
Async XLA Ops:
  7.2 10.6 copy-start.28
  7.2 88.8 %all-gather.2.cloned.1.call-start = ((), (), s32[]{:S(2)}) async-start(), calls=%async_computation.1 | async-start | bytes 4866048 | tf_op jit(solution)/shard_map/all_gather | solution.py:73
  7.9 1054.5 %reduce-scatter.2.cloned.1.call-start = ((), (), s32[]{:S(2)}) async-start(), calls=%async_computation.2 | async-start | bytes 4866048 | tf_op jit(solution)/shard_map/reduce_scatter | solution.py:123
  11.0 11.8 %collective-permute-start = (bf16[128,1536]{1,0:T(8,128)(2,1)S(1)}, bf16[128,1536]{1,0:T(8,128)(2,1)S(1)}, u32[]{:S(2)}, u32[]{:S(2)}) collective-permute-start(bf16[128,1536]{1,0:T(8,128)(2,1)S(1)} %fusion.570), channel_id=1, source_target_pairs={{0,1},{1,2},{2,3},{4,5},{5,6},{6,7},{8,9},{9,10},{10,11},{12,13},{... | collective-permute-start | bytes 1179656 | tf_op jit(solution)/shard_map/ppermute | solution.py:16
  22.9 73.0 %copy-start.30 = (f32[1,1536]{1,0:T(1,128)S(1)}, f32[1,1536]{1,0:T(1,128)}, u32[]{:S(2)}) copy-start(f32[1,1536]{1,0:T(1,128)} %param.42) | copy-start | bytes 18436
  22.9 73.0 %copy-start.40 = (pred[256]{0:T(512)(128)(4,1)S(1)}, pred[256]{0:T(512)(128)(4,1)}, u32[]{:S(2)}) copy-start(pred[256]{0:T(512)(128)(4,1)} %concatenate.6) | copy-start | bytes 772
  96.0 10.9 %copy-start = (bf16[1,1,128,1536]{3,2,1,0:T(8,128)(2,1)S(1)}, bf16[1,1,128,1536]{3,2,1,0:T(8,128)(2,1)}, u32[]{:S(2)}) copy-start(bf16[1,1,128,1536]{3,2,1,0:T(8,128)(2,1)} %param.39) | copy-start | bytes 1179652
  96.8 10.3 copy-start.29
  96.9 10.3 copy-start.32
  96.9 10.0 collective-permute-start.1
  107.5 3.7 collective-permute-start.2
  111.6 9.7 collective-permute-start.3
  123.1 7.3 collective-permute-start.4
  132.2 10.3 copy-start.10
  132.2 10.0 collective-permute-start.5
  143.6 10.9 %collective-permute-start.6 = (bf16[128,1536]{1,0:T(8,128)(2,1)}, bf16[128,1536]{1,0:T(8,128)(2,1)S(1)}, u32[]{:S(2)}, u32[]{:S(2)}) collective-permute-start(bf16[128,1536]{1,0:T(8,128)(2,1)} %fusion.585), channel_id=1, source_target_pairs={{32,0},{64,32},{96,64},{128,96},{160,128},{192,160},{224,192},{33,... | collective-permute-start | bytes 1179656 | tf_op jit(solution)/shard_map/ppermute | solution.py:16
  157.2 10.3 copy-start.12
  157.2 10.0 collective-permute-start.7
  168.6 9.7 collective-permute-start.8
  181.0 10.3 copy-start.14
  181.0 10.0 collective-permute-start.9
  192.4 9.4 collective-permute-start.10
  204.8 10.3 copy-start.16
  204.8 10.0 collective-permute-start.11
  216.2 8.1 collective-permute-start.12
  226.9 10.3 copy-start.18
  227.0 10.0 collective-permute-start.13
  238.4 316.3 %collective-permute-start.14 = (bf16[128,1536]{1,0:T(8,128)(2,1)}, bf16[128,1536]{1,0:T(8,128)(2,1)}, u32[]{:S(2)}, u32[]{:S(2)}) collective-permute-start(bf16[128,1536]{1,0:T(8,128)(2,1)} %fusion.581), channel_id=1, source_target_pairs={{32,0},{64,32},{96,64},{128,96},{160,128},{192,160},{224,192},{33,... | collective-permute-start | bytes 1179656 | tf_op jit(solution)/shard_map/ppermute | solution.py:16
  640.3 10.3 copy-start.8
  640.3 10.3 copy-start.27
  640.4 10.3 copy-start.39
  640.4 10.0 collective-permute-start.15
  (16 other events, 88.9 us)
Sparse Core Ops, SparseCore 0:
  10.6 85.3 all-gather.1
  640.5 421.9 reduce-scatter.1
where the time goes:
time: 1080 us; the launch traced here: 1070 us
  waiting for transfers between devices  908 us (84%)
  matrix products  72.3 us (7%)
  local copies, waits for them, and re-layouts  25.1 us (2%)
  starting transfers between devices  23.8 us (2%)
  between operations  21 us (2%)
  other arithmetic  17.7 us (2%)
    ppermute x16, waiting for transfers between devices, from_behind(): lax.ppermute(value, axis, [(source, source + steps) for source in range(i...  425 us
    reduce_scatter x1, waiting for transfers between devices, per_device(): lax.psum_scatter(lax.dot_general(normed, kept_grad, (((0,), (0,)), ((), (...  409 us
    all_gather x1, waiting for transfers between devices, per_device(): weights = lax.all_gather(w_query, ('fsdp', 'seq'), axis=1, tiled=True)[0]  72.7 us
    ppermute x16, starting transfers between devices, from_behind(): lax.ppermute(value, axis, [(source, source + steps) for source in range(i...  23.7 us
  transfers between devices with their start and end apart: 18, of which 18 were waited for; matrix products, arithmetic and copies ran while one was open for 1% of the time, Pallas kernels for 0%

commit v1 on v0

v1 whole, which is shorter than its diff:
```python
import functools
import jax
import jax.numpy as jnp
from jax import lax
from jax.experimental import pallas as pl
from jax.experimental.pallas import tpu as pltpu
from jax.sharding import PartitionSpec as P

HDIM = 128
GROUP = 256
norm_eps = 1e-06
MESH = pl.DeviceIdType.MESH
NN = (((1,), (0,)), ((), ()))
NT = (((1,), (1,)), ((), ()))


def mm(a, b, dims=NN):
    return lax.dot_general(a, b, dims, preferred_element_type=jnp.float32)


def chain_kernel(
    x_ref, go_ref, gain_ref, gate_ref, w_ref, kept_ref, links_ref,
    out_ref, qg_ref, normed_ref,
    keys, inv_s, q_s, pt_s, kt_s, dy_buf, lr_send, lr_recv, kgo_s, ng_s, qg_s,
    nsend, nrecv, lsend, lrecv, dsend, drecv,
):
    sections = lax.axis_size("section")
    tiles = lax.axis_size("seq")
    sec = lax.axis_index("section")
    seq = lax.axis_index("seq")
    fsdp = lax.axis_index("fsdp")
    rows, width = x_ref.shape
    heads = width // HDIM
    groups = width // GROUP
    per_group = GROUP // HDIM
    scale = HDIM ** (-0.5)

    barrier = pltpu.get_barrier_semaphore()
    for other in (
        (lax.rem(sec + 1, sections), fsdp, seq),
        (lax.rem(sec + sections - 1, sections), fsdp, seq),
        (sec, fsdp, lax.rem(seq + 1, tiles)),
        (sec, fsdp, lax.rem(seq + tiles - 1, tiles)),
    ):
        pl.semaphore_signal(barrier, inc=1, device_id=other, device_id_type=MESH)

    keep = kept_ref[0, sec]
    linked = links_ref[0, 0] * jnp.minimum(seq, 1)

    def norm_block(step, carry):
        at = pl.ds(pl.multiple_of(step * 16, 16), 16)
        x_rows = x_ref[at, :].astype(jnp.float32)
        inv = lax.rsqrt(jnp.mean(x_rows * x_rows, axis=-1, keepdims=True) + norm_eps)
        inv_s[at, :] = jnp.broadcast_to(inv, (16, 128))
        rounded = (x_rows * inv * gain_ref[...]).astype(jnp.bfloat16)
        normed_ref[at, :] = rounded
        keys[pl.ds(pl.multiple_of(rows + step * 16, 16), 16), :] = rounded
        return carry

    lax.fori_loop(0, rows // 16, norm_block, 0)

    @pl.when(seq == 0)
    def _():
        keys[0:rows, :] = jnp.zeros((rows, width), jnp.bfloat16)

    @pl.when(seq == tiles - 1)
    def _():
        lr_recv[...] = jnp.zeros_like(lr_recv)

    pl.semaphore_wait(barrier, 4)

    left_copy = pltpu.make_async_remote_copy(
        src_ref=keys.at[pl.ds(rows, rows), :],
        dst_ref=keys.at[pl.ds(0, rows), :],
        send_sem=nsend,
        recv_sem=nrecv,
        device_id=(sec, fsdp, lax.rem(seq + 1, tiles)),
        device_id_type=MESH,
    )

    @pl.when(seq < tiles - 1)
    def _():
        left_copy.start()

    def query_block(step, carry):
        at = pl.ds(pl.multiple_of(step * GROUP, GROUP), GROUP)
        q_s[:, at] = mm(normed_ref[...], w_ref[:, at]).astype(jnp.bfloat16)
        return carry

    lax.fori_loop(0, groups, query_block, 0)

    @pl.when(seq > 0)
    def _():
        left_copy.wait_recv()

    @pl.when(seq < tiles - 1)
    def _():
        left_copy.wait_send()

    def probs_block(head, carry):
        at = pl.ds(pl.multiple_of(head * HDIM, HDIM), HDIM)
        key_part = keys[:, at]
        scores = mm(key_part, q_s[:, at], NT) * scale
        position = lax.broadcasted_iota(jnp.int32, scores.shape, 0)
        valid = position + linked * rows >= rows
        scores = jnp.where(valid, scores, -1e30)
        top = jnp.max(scores, axis=0, keepdims=True)
        weight = jnp.exp(scores - top)
        pt_s[head] = weight / jnp.sum(weight, axis=0, keepdims=True)
        kt_s[head] = key_part.T
        return carry

    lax.fori_loop(0, heads, probs_block, 0)

    @pl.when(sec == sections - 1)
    def _():
        dy_buf[...] = go_ref[...]

    def dy_copy(group):
        at = pl.ds(group * GROUP, GROUP)
        return pltpu.make_async_remote_copy(
            src_ref=out_ref.at[:, at],
            dst_ref=dy_buf.at[:, at],
            send_sem=dsend.at[group],
            recv_sem=drecv.at[group],
            device_id=(lax.rem(sec + sections - 1, sections), fsdp, seq),
            device_id_type=MESH,
        )

    def lr_copy(group):
        at = pl.ds(group * GROUP, GROUP)
        return pltpu.make_async_remote_copy(
            src_ref=lr_send.at[:, at],
            dst_ref=lr_recv.at[:, at],
            send_sem=lsend.at[group],
            recv_sem=lrecv.at[group],
            device_id=(sec, fsdp, lax.rem(seq + tiles - 1, tiles)),
            device_id_type=MESH,
        )

    def attention(group):
        for head in range(group * per_group, (group + 1) * per_group):
            at = pl.ds(head * HDIM, HDIM)
            grad = (gate_ref[:, at] * dy_buf[:, at].astype(jnp.float32)).astype(jnp.bfloat16)
            probs = pt_s[head]
            prob_grad = mm(keys[:, at], grad, NT)
            delta = jnp.sum(probs * prob_grad, axis=0, keepdims=True)
            score_grad = (probs * (prob_grad - delta) * scale).astype(jnp.bfloat16)
            key_grad = mm(
                jnp.concatenate([score_grad, probs.astype(jnp.bfloat16)], axis=1),
                jnp.concatenate([q_s[:, at], grad], axis=0),
            )
            lr_send[:, at] = key_grad[:rows].astype(jnp.bfloat16)
            kgo_s[:, at] = key_grad[rows:]
            qg_s[:, at] = mm(kt_s[head], score_grad).astype(jnp.bfloat16).T

    def project(group):
        at = pl.ds(group * GROUP, GROUP)
        part = mm(qg_s[:, at], w_ref[:, at], NT)
        if group == 0:
            ng_s[...] = part
        else:
            ng_s[...] += part

    for group in range(groups):

        @pl.when(sec < sections - 1)
        def _():
            dy_copy(group).wait_recv()

        attention(group)

        @pl.when(seq > 0)
        def _():
            lr_copy(group).start()

        if group > 0:
            project(group - 1)
    project(groups - 1)

    @pl.when(seq < tiles - 1)
    def _():
        for group in range(groups):
            lr_copy(group).wait_recv()

    def finish_block(step, carry):
        at = pl.ds(pl.multiple_of(step * 16, 16), 16)
        x_rows = x_ref[at, :].astype(jnp.float32)
        inv = inv_s[at, 0:1]
        total = ng_s[at, :] + kgo_s[at, :] + lr_recv[at, :].astype(jnp.float32)
        total = total * gain_ref[...]
        mean_term = jnp.mean(x_rows * total, axis=-1, keepdims=True)
        change = inv * (total - x_rows * (inv * inv * mean_term))
        before = dy_buf[at, :].astype(jnp.float32)
        kept_here = jnp.full(before.shape, keep, jnp.int32) > 0
        out_ref[at, :] = jnp.where(kept_here, before + change, before).astype(jnp.bfloat16)
        return carry

    lax.fori_loop(0, rows // 16, finish_block, 0)

    @pl.when(sec > 0)
    def _():
        for group in range(groups):
            dy_copy(group).start()

    grads = qg_s[...].astype(jnp.float32)
    qg_ref[...] = jnp.where(
        jnp.full(grads.shape, keep, jnp.int32) > 0, grads, jnp.zeros_like(grads)
    ).astype(jnp.bfloat16)

    @pl.when(seq > 0)
    def _():
        for group in range(groups):
            lr_copy(group).wait_send()

    @pl.when(sec > 0)
    def _():
        for group in range(groups):
            dy_copy(group).wait_send()


def run_chain(x, grad_out, gain, gate, weights, kept, links):
    rows, width = x.shape
    heads = width // HDIM
    groups = width // GROUP
    vmem = pl.BlockSpec(memory_space=pltpu.VMEM)
    smem = pl.BlockSpec(memory_space=pltpu.SMEM)
    low = jnp.bfloat16
    block = jax.ShapeDtypeStruct((rows, width), low)
    return pl.pallas_call(
        chain_kernel,
        out_shape=(block, block, block),
        in_specs=[vmem] * 5 + [smem] * 2,
        out_specs=(vmem, vmem, vmem),
        scratch_shapes=[
            pltpu.VMEM((2 * rows, width), low),
            pltpu.VMEM((rows, 128), jnp.float32),
            pltpu.VMEM((rows, width), low),
            pltpu.VMEM((heads, 2 * rows, rows), jnp.float32),
            pltpu.VMEM((heads, HDIM, 2 * rows), low),
            pltpu.VMEM((rows, width), low),
            pltpu.VMEM((rows, width), low),
            pltpu.VMEM((rows, width), low),
            pltpu.VMEM((rows, width), jnp.float32),
            pltpu.VMEM((rows, width), jnp.float32),
            pltpu.VMEM((rows, width), low),
            pltpu.SemaphoreType.DMA,
            pltpu.SemaphoreType.DMA,
            pltpu.SemaphoreType.DMA((groups,)),
            pltpu.SemaphoreType.DMA((groups,)),
            pltpu.SemaphoreType.DMA((groups,)),
            pltpu.SemaphoreType.DMA((groups,)),
        ],
        compiler_params=pltpu.CompilerParams(
            collective_id=0, has_side_effects=True, vmem_limit_bytes=56 * 2**20
        ),
        name="chain",
    )(x, grad_out, gain, gate, weights, kept, links)


def per_device(acts, grad_out, gain, gate, w_query, kept, links):
    weights = lax.all_gather(w_query[0], ("fsdp", "seq"), axis=0, tiled=True)
    result, query_grad, normed = run_chain(
        acts[0, 0], grad_out[0], gain, gate, weights, kept, links
    )
    grad_rows = lax.psum_scatter(
        lax.dot_general(
            normed, query_grad, (((0,), (0,)), ((), ())), preferred_element_type=jnp.float32
        ).astype(jnp.bfloat16),
        ("fsdp", "seq"),
        scatter_dimension=0,
        tiled=True,
    )
    return (result[None, None], grad_rows[None])


def solution(mesh):
    placed = (
        P("section", "fsdp", "seq", None),
        P("fsdp", "seq", None),
        P("section", None),
        P("section", None),
        P("section", ("fsdp", "seq"), None),
        P("fsdp", None),
        P("fsdp", "seq"),
    )
    return jax.shard_map(
        per_device,
        mesh=mesh,
        in_specs=placed,
        out_specs=(P("section", "fsdp", "seq", None), P("section", ("fsdp", "seq"), None)),
        check_vma=False,
    )
```

time: 1080 us -> 426 us (0.39)
  waiting for transfers between devices: 908 us -> 307 us
  Pallas kernels: 0 us -> 97.1 us
  matrix products: 72.3 us -> 4.71 us
  local copies, waits for them, and re-layouts: 25.1 us -> 0.75 us
  starting transfers between devices: 23.8 us -> 0.08 us
  other arithmetic: 17.7 us -> 0 us
    ppermute x16 -> x0, waiting for transfers between devices: 425 us -> none  [from_behind(): lax.ppermute(value, axis, [(source, source + steps) for source in range(i...]
    reduce_scatter x1, waiting for transfers between devices: 409 us -> 219 us  [per_device(): lax.psum_scatter(lax.dot_general(normed, query_grad, (((0,), (0,)), ((),...]
    pallas_call x0 -> x1, Pallas kernels: none -> 97.1 us  [run_chain(): pl.pallas_call(chain_kernel, out_shape=(block, block, block), in_specs=[v...]
    dot_general x27 -> x1, matrix products: 66.4 us -> 4.71 us  [per_device(): lax.dot_general(normed, query_grad, (((0,), (0,)), ((), ())), preferred_e...]
    ppermute x16 -> x0, starting transfers between devices: 23.7 us -> none  [from_behind(): lax.ppermute(value, axis, [(source, source + steps) for source in range(i...]
    all_gather x1, waiting for transfers between devices: 72.7 us -> 87.3 us  [per_device(): weights = lax.all_gather(w_query[0], ('fsdp', 'seq'), axis=0, tiled=True)]
  transfers between devices with their start and end apart: 18 -> 2, of which waited for: 18 -> 2; matrix products, arithmetic and copies ran while one was open for 1% -> 0% of each run, Pallas kernels for 0% -> 0%
where the time goes in v1:
time: 426 us; the launch traced here: 425 us
  waiting for transfers between devices  307 us (72%)
  Pallas kernels  97.1 us (23%)
  between operations  14.7 us (3%)
  matrix products  4.71 us (1%)
    reduce_scatter x1, waiting for transfers between devices, per_device(): lax.psum_scatter(lax.dot_general(normed, query_grad, (((0,), (0,)), ((),...  219 us
    pallas_call x1, Pallas kernels, run_chain(): pl.pallas_call(chain_kernel, out_shape=(block, block, block), in_specs=[v...  97.1 us
    all_gather x1, waiting for transfers between devices, per_device(): weights = lax.all_gather(w_query[0], ('fsdp', 'seq'), axis=0, tiled=True)  87.3 us
  transfers between devices with their start and end apart: 2, of which 2 were waited for; matrix products, arithmetic and copies ran while one was open for 0% of the time, Pallas kernels for 0%

profile of v1, /device:TPU:32, one launch (start us, length us, event | category | flops | bytes accessed | tf_op | source)
XLA Modules:
  0.0 424.8 jit_solution(10912500493815283041)
XLA Ops:
  7.2 0.0 all-gather.3.cloned.1.call-start
  7.2 0.7 all-gather.3.cloned.1.call-update
  7.9 0.0 reduce-scatter.2.cloned.1.call-start
  8.6 87.3 %all-gather.3.cloned.1.call-done = bf16[1,1536,1536]{2,1,0:T(8,128)(2,1)} async-done(((bf16[1,48,1536]{2,1,0:T(8,128)(2,1)}), bf16[1,1536,1536]{2,1,0:T(8,128)(2,1)}) %all-gather.3.cloned.1.call-update) | async-done | bytes 4718608 | tf_op jit(solution)/shard_map/all_gather | solution.py:262
  95.9 97.1 %chain.1 = (bf16[128,1536]{1,0:T(8,128)(2,1)}, bf16[128,1536]{1,0:T(8,128)(2,1)}, bf16[128,1536]{1,0:T(8,128)(2,1)}) custom-call(bf16[128,1536]{1,0:T(8,128)(2,1)} %bitcast.9, bf16[128,1536]{1,0:T(8,128)(2,1)} %bitcast.10, f32[1,1536]{1,0:T(1,128)} %gain_ref.1, f32[1,1536]{1,0:T(1,128)} %gate_ref.1, bf16[1536,1536]{1,0:T(8,128)(2,1)} %bitcast.7, ...), custom_call_target="tpu_custom_call" | custom-call | tf_op jit(solution)/shard_map/chain/pallas_call | solution.py:230
  193.1 0.0 copy-start
  193.1 4.7 %convolution_convert_fusion = bf16[1536,1536]{1,0:T(8,128)(2,1)} fusion(bf16[128,1536]{1,0:T(8,128)(2,1)} %get-tuple-element.6, bf16[128,1536]{1,0:T(8,128)(2,1)} %get-tuple-element.7), kind=kOutput, calls=%fused_computation | convolution fusion | flops 606339072 | bytes 5505024 | tf_op jit(solution)/shard_map/dot_general | solution.py:267
  197.8 0.0 reduce-scatter.2.cloned.1.call-update
  197.8 219.4 %reduce-scatter.2.cloned.1.call-done = bf16[48,1536]{1,0:T(8,128)(2,1)} async-done(((bf16[1536,1536]{1,0:T(8,128)(2,1)}), bf16[48,1536]{1,0:T(8,128)(2,1)}) %reduce-scatter.2.cloned.1.call-update) | async-done | bytes 147472 | tf_op jit(solution)/shard_map/reduce_scatter | solution.py:266
  417.2 0.0 copy-done
  417.2 0.7 copy.11
Async XLA Ops:
  7.2 88.8 %all-gather.3.cloned.1.call-start = ((), (), s32[]{:S(2)}) async-start(), calls=%async_computation.2 | async-start | bytes 4866048 | tf_op jit(solution)/shard_map/all_gather | solution.py:262
  7.9 409.3 %reduce-scatter.2.cloned.1.call-start = ((), (), s32[]{:S(2)}) async-start(), calls=%async_computation.1 | async-start | bytes 4866048 | tf_op jit(solution)/shard_map/reduce_scatter | solution.py:266
  193.1 224.1 %copy-start = (bf16[128,1536]{1,0:T(8,128)(2,1)S(1)}, bf16[128,1536]{1,0:T(8,128)(2,1)}, u32[]{:S(2)}) copy-start(bf16[128,1536]{1,0:T(8,128)(2,1)} %get-tuple-element.5) | copy-start | bytes 1179652
Sparse Core Ops, SparseCore 0:
  10.6 85.3 all-gather.2
  198.0 219.1 reduce-scatter.1

commit v2 on v1

--- a/solution.py
+++ b/solution.py
@@ -1,4 +1,3 @@
-import functools
 import jax
 import jax.numpy as jnp
 from jax import lax
@@ -18,10 +17,125 @@
     return lax.dot_general(a, b, dims, preferred_element_type=jnp.float32)
 
 
+LINK_RATE = 85e3
+HOP_TIME = 1.7
+BLOCK_TIME = 0.6
+
+
+def hops_of(size, flip):
+    far, near = size // 2, size - 1 - size // 2
+    return ((1, near), (-1, far)) if flip else ((1, far), (-1, near))
+
+
+def spread_plan(size_z, size_y):
+    plan = []
+    sizes = (size_z, size_y)
+    for part, first in ((1, 0), (0, 1)):
+        second = 1 - first
+        held = [(0, None)]
+        for sign, hops in hops_of(sizes[first], False):
+            before = None
+            for hop in range(1, hops + 1):
+                block = [0, 0]
+                block[first] = -sign * (hop - 1)
+                plan.append((first, sign, tuple(block), part, [] if before is None else [before]))
+                before = len(plan) - 1
+                held.append((-sign * hop, before))
+        for stream, (offset, source) in enumerate(held):
+            for sign, hops in hops_of(sizes[second], stream % 2 == 1):
+                before = source
+                for hop in range(1, hops + 1):
+                    block = [0, 0]
+                    block[first] = offset
+                    block[second] = -sign * (hop - 1)
+                    plan.append(
+                        (second, sign, tuple(block), part, [] if before is None else [before])
+                    )
+                    before = len(plan) - 1
+    return plan
+
+
+def far_first(size):
+    order = []
+    for sign, hops in hops_of(size, False):
+        order += [sign * hop for hop in range(1, hops + 1)]
+    return sorted(order, key=lambda step: (-abs(step), -step)) + [0]
+
+
+def sum_plan(size_z, size_y):
+    plan, ends = [], {}
+    sizes = (size_z, size_y)
+    for part, first in ((0, 0), (1, 1)):
+        second = 1 - first
+        landed = {}
+        for stream, offset in enumerate(far_first(sizes[second])):
+            landed[offset % sizes[second]] = last = []
+            for sign, hops in hops_of(sizes[first], stream % 2 == 1):
+                for hop in range(1, hops + 1):
+                    block = [0, 0]
+                    block[second] = offset
+                    block[first] = sign * (hops + 1 - hop)
+                    plan.append(
+                        (first, sign, tuple(block), part, [] if hop == 1 else [len(plan) - 1])
+                    )
+                if hops:
+                    last.append(len(plan) - 1)
+        last = list(landed[0])
+        for sign, hops in hops_of(sizes[second], False):
+            for hop in range(1, hops + 1):
+                block = [0, 0]
+                block[second] = sign * (hops + 1 - hop)
+                adds = list(landed[block[second] % sizes[second]])
+                plan.append(
+                    (second, sign, tuple(block), part, adds + ([] if hop == 1 else [len(plan) - 1]))
+                )
+            if hops:
+                last.append(len(plan) - 1)
+        ends[part] = last
+    return plan, ends
+
+
+def run_plan(plan, part_bytes, ready):
+    free, arrival, events = {}, {}, []
+    done, started, now = set(), set(), 0.0
+    made = set()
+    todo = list(ready)
+
+    def launch():
+        for index, (axis, sign, block, part, deps) in enumerate(plan):
+            if index in started or any(dep not in done for dep in deps):
+                continue
+            if ready and block[0] not in made:
+                continue
+            started.add(index)
+            begin = max(now, free.get((axis, sign), 0.0))
+            free[axis, sign] = begin + part_bytes[part] / LINK_RATE
+            arrival[index] = free[axis, sign] + HOP_TIME
+            events.append(("start", index))
+
+    launch()
+    while len(done) < len(plan):
+        coming = sorted((when, index) for index, when in arrival.items() if index not in done)
+        if todo and (not coming or coming[0][0] > now):
+            step = todo.pop(0)
+            events.append(("make", step))
+            made.update(step)
+            now += BLOCK_TIME
+        else:
+            when, index = coming[0]
+            now = max(now, when)
+            done.add(index)
+            events.append(("wait", index))
+        launch()
+    return events
+
+
 def chain_kernel(
-    x_ref, go_ref, gain_ref, gate_ref, w_ref, kept_ref, links_ref,
-    out_ref, qg_ref, normed_ref,
+    x_ref, go_ref, gain_ref, gate_ref, shard_ref, kept_ref, links_ref,
+    out_ref, grad_ref,
+    w_ref, wgrad, slots_a, slots_b,
     keys, inv_s, q_s, pt_s, kt_s, dy_buf, lr_send, lr_recv, kgo_s, ng_s, qg_s,
+    own_sem, turn, gsend, grecv, ssend, srecv,
     nsend, nrecv, lsend, lrecv, dsend, drecv,
 ):
     sections = lax.axis_size("section")
@@ -34,6 +148,21 @@
     groups = width // GROUP
     per_group = GROUP // HDIM
     scale = HDIM ** (-0.5)
+    ring_z = lax.axis_size("fsdp")
+    shard = width // (ring_z * tiles)
+    cut = first_columns(width)
+    columns = (pl.ds(0, cut), pl.ds(cut, width - cut))
+    part_bytes = (2 * shard * cut, 2 * shard * (width - cut))
+
+    def neighbour(axis, sign):
+        if axis == 0:
+            return (sec, lax.rem(fsdp + sign + ring_z, ring_z), seq)
+        return (sec, fsdp, lax.rem(seq + sign + tiles, tiles))
+
+    def rows_of(block):
+        at_z = lax.rem(fsdp + block[0] + ring_z, ring_z)
+        at_y = lax.rem(seq + block[1] + tiles, tiles)
+        return pl.ds(pl.multiple_of((at_z * tiles + at_y) * shard, shard), shard)
 
     barrier = pltpu.get_barrier_semaphore()
     for other in (
@@ -41,9 +170,13 @@
         (lax.rem(sec + sections - 1, sections), fsdp, seq),
         (sec, fsdp, lax.rem(seq + 1, tiles)),
         (sec, fsdp, lax.rem(seq + tiles - 1, tiles)),
+        (sec, lax.rem(fsdp + 1, ring_z), seq),
+        (sec, lax.rem(fsdp + ring_z - 1, ring_z), seq),
     ):
         pl.semaphore_signal(barrier, inc=1, device_id=other, device_id_type=MESH)
 
+    own_copy = pltpu.make_async_copy(shard_ref, w_ref.at[rows_of((0, 0)), :], own_sem)
+    own_copy.start()
     keep = kept_ref[0, sec]
     linked = links_ref[0, 0] * jnp.minimum(seq, 1)
 
@@ -53,7 +186,6 @@
         inv = lax.rsqrt(jnp.mean(x_rows * x_rows, axis=-1, keepdims=True) + norm_eps)
         inv_s[at, :] = jnp.broadcast_to(inv, (16, 128))
         rounded = (x_rows * inv * gain_ref[...]).astype(jnp.bfloat16)
-        normed_ref[at, :] = rounded
         keys[pl.ds(pl.multiple_of(rows + step * 16, 16), 16), :] = rounded
         return carry
 
@@ -67,7 +199,8 @@
     def _():
         lr_recv[...] = jnp.zeros_like(lr_recv)
 
-    pl.semaphore_wait(barrier, 4)
+    pl.semaphore_wait(barrier, 6)
+    own_copy.wait()
 
     left_copy = pltpu.make_async_remote_copy(
         src_ref=keys.at[pl.ds(rows, rows), :],
@@ -82,9 +215,44 @@
     def _():
         left_copy.start()
 
+    gather = spread_plan(ring_z, tiles)
+
+    def gather_copy(index):
+        axis, sign, block, part, _ = gather[index]
+        place = w_ref.at[rows_of(block), columns[part]]
+        return pltpu.make_async_remote_copy(
+            src_ref=place,
+            dst_ref=place,
+            send_sem=gsend.at[index],
+            recv_sem=grecv.at[index],
+            device_id=neighbour(axis, sign),
+            device_id_type=MESH,
+        )
+
+    if sections % 2 == 0:
+
+        @pl.when(lax.rem(sec, 2) == 0)
+        def _():
+            pl.semaphore_wait(turn, 1)
+
+    for kind, index in run_plan(gather, part_bytes, ()):
+        if kind == "start":
+            gather_copy(index).start()
+        else:
+            gather_copy(index).wait_recv()
+    for index in range(len(gather)):
+        gather_copy(index).wait_send()
+    if sections % 2 == 0:
+
+        @pl.when(lax.rem(sec, 2) == 1)
+        def _():
+            pl.semaphore_signal(
+                turn, inc=1, device_id=(sec - 1, fsdp, seq), device_id_type=MESH
+            )
+
     def query_block(step, carry):
         at = pl.ds(pl.multiple_of(step * GROUP, GROUP), GROUP)
-        q_s[:, at] = mm(normed_ref[...], w_ref[:, at]).astype(jnp.bfloat16)
+        q_s[:, at] = mm(keys[rows:, :], w_ref[:, at]).astype(jnp.bfloat16)
         return carry
 
     lax.fori_loop(0, groups, query_block, 0)
@@ -107,7 +275,7 @@
         top = jnp.max(scores, axis=0, keepdims=True)
         weight = jnp.exp(scores - top)
         pt_s[head] = weight / jnp.sum(weight, axis=0, keepdims=True)
-        kt_s[head] = key_part.T
+        kt_s[at, :] = key_part.T
         return carry
 
     lax.fori_loop(0, heads, probs_block, 0)
@@ -152,7 +320,7 @@
             )
             lr_send[:, at] = key_grad[:rows].astype(jnp.bfloat16)
             kgo_s[:, at] = key_grad[rows:]
-            qg_s[:, at] = mm(kt_s[head], score_grad).astype(jnp.bfloat16).T
+            qg_s[:, at] = mm(kt_s[at, :], score_grad).astype(jnp.bfloat16).T
 
     def project(group):
         at = pl.ds(group * GROUP, GROUP)
@@ -204,10 +372,61 @@
             dy_copy(group).start()
 
     grads = qg_s[...].astype(jnp.float32)
-    qg_ref[...] = jnp.where(
+    qg_s[...] = jnp.where(
         jnp.full(grads.shape, keep, jnp.int32) > 0, grads, jnp.zeros_like(grads)
     ).astype(jnp.bfloat16)
 
+    sums, ends = sum_plan(ring_z, tiles)
+    slot_refs = (slots_a, slots_b)
+    slot_at, used = {}, [0, 0]
+    for index, (_, _, _, part, _) in enumerate(sums):
+        slot_at[index] = used[part]
+        used[part] += 1
+
+    def sum_copy(index):
+        axis, sign, block, part, _ = sums[index]
+        return pltpu.make_async_remote_copy(
+            src_ref=wgrad.at[rows_of(block), columns[part]],
+            dst_ref=slot_refs[part].at[slot_at[index]],
+            send_sem=ssend.at[index],
+            recv_sem=srecv.at[index],
+            device_id=neighbour(axis, sign),
+            device_id_type=MESH,
+        )
+
+    def summed(block, part, adds):
+        total = wgrad[rows_of(block), columns[part]].astype(jnp.float32)
+        for index in adds:
+            total = total + slot_refs[part][slot_at[index]].astype(jnp.float32)
+        return total.astype(jnp.bfloat16)
+
+    def make(offset):
+        span = tiles * shard
+        start = lax.rem(fsdp + offset + ring_z, ring_z) * span
+        at = pl.ds(pl.multiple_of(start, shard), span)
+        left = kt_s[at, rows : 2 * rows]
+        for group in range(groups):
+            to = pl.ds(group * GROUP, GROUP)
+            wgrad[at, to] = mm(left, qg_s[:, to]).astype(jnp.bfloat16)
+
+    makes = []
+    for offset in far_first(ring_z):
+        makes.append((offset, offset - ring_z, offset + ring_z))
+    for kind, index in run_plan(sums, part_bytes, makes):
+        if kind == "make":
+            make(index[0])
+        elif kind == "start":
+            _, _, block, part, adds = sums[index]
+            if adds:
+                wgrad[rows_of(block), columns[part]] = summed(block, part, adds)
+            sum_copy(index).start()
+        else:
+            sum_copy(index).wait_recv()
+    for part in (0, 1):
+        grad_ref[:, columns[part]] = summed((0, 0), part, ends[part])
+    for index in range(len(sums)):
+        sum_copy(index).wait_send()
+
     @pl.when(seq > 0)
     def _():
         for group in range(groups):
@@ -219,57 +438,67 @@
             dy_copy(group).wait_send()
 
 
-def run_chain(x, grad_out, gain, gate, weights, kept, links):
+def first_columns(width):
+    return max(1, round(width * 5 / 12 / 128)) * 128
+
+
+def run_chain(x, grad_out, gain, gate, shard, kept, links):
     rows, width = x.shape
     heads = width // HDIM
     groups = width // GROUP
     vmem = pl.BlockSpec(memory_space=pltpu.VMEM)
     smem = pl.BlockSpec(memory_space=pltpu.SMEM)
     low = jnp.bfloat16
-    block = jax.ShapeDtypeStruct((rows, width), low)
+    count = lax.axis_size("fsdp") * lax.axis_size("seq") - 1
+    cut = first_columns(width)
+    dma = pltpu.SemaphoreType.DMA
     return pl.pallas_call(
         chain_kernel,
-        out_shape=(block, block, block),
+        out_shape=(
+            jax.ShapeDtypeStruct((rows, width), low),
+            jax.ShapeDtypeStruct(shard.shape, low),
+        ),
         in_specs=[vmem] * 5 + [smem] * 2,
-        out_specs=(vmem, vmem, vmem),
+        out_specs=(vmem, vmem),
         scratch_shapes=[
+            pltpu.VMEM((width, width), low),
+            pltpu.VMEM((width, width), low),
+            pltpu.VMEM((count, shard.shape[0], cut), low),
+            pltpu.VMEM((count, shard.shape[0], width - cut), low),
             pltpu.VMEM((2 * rows, width), low),
             pltpu.VMEM((rows, 128), jnp.float32),
             pltpu.VMEM((rows, width), low),
             pltpu.VMEM((heads, 2 * rows, rows), jnp.float32),
-            pltpu.VMEM((heads, HDIM, 2 * rows), low),
+            pltpu.VMEM((width, 2 * rows), low),
             pltpu.VMEM((rows, width), low),
             pltpu.VMEM((rows, width), low),
             pltpu.VMEM((rows, width), low),
             pltpu.VMEM((rows, width), jnp.float32),
             pltpu.VMEM((rows, width), jnp.float32),
             pltpu.VMEM((rows, width), low),
-            pltpu.SemaphoreType.DMA,
-            pltpu.SemaphoreType.DMA,
-            pltpu.SemaphoreType.DMA((groups,)),
-            pltpu.SemaphoreType.DMA((groups,)),
-            pltpu.SemaphoreType.DMA((groups,)),
-            pltpu.SemaphoreType.DMA((groups,)),
+            dma,
+            pltpu.SemaphoreType.REGULAR,
+            dma((2 * count,)),
+            dma((2 * count,)),
+            dma((2 * count,)),
+            dma((2 * count,)),
+            dma,
+            dma,
+            dma((groups,)),
+            dma((groups,)),
+            dma((groups,)),
+            dma((groups,)),
         ],
         compiler_params=pltpu.CompilerParams(
             collective_id=0, has_side_effects=True, vmem_limit_bytes=56 * 2**20
         ),
         name="chain",
-    )(x, grad_out, gain, gate, weights, kept, links)
+    )(x, grad_out, gain, gate, shard, kept, links)
 
 
 def per_device(acts, grad_out, gain, gate, w_query, kept, links):
-    weights = lax.all_gather(w_query[0], ("fsdp", "seq"), axis=0, tiled=True)
-    result, query_grad, normed = run_chain(
-        acts[0, 0], grad_out[0], gain, gate, weights, kept, links
-    )
-    grad_rows = lax.psum_scatter(
-        lax.dot_general(
-            normed, query_grad, (((0,), (0,)), ((), ())), preferred_element_type=jnp.float32
-        ).astype(jnp.bfloat16),
-        ("fsdp", "seq"),
-        scatter_dimension=0,
-        tiled=True,
+    result, grad_rows = run_chain(
+        acts[0, 0], grad_out[0], gain, gate, w_query[0], kept, links
     )
     return (result[None, None], grad_rows[None])
 

time: 426 us -> 189 us (0.44)
  waiting for transfers between devices: 307 us -> 0 us
  Pallas kernels: 97.1 us -> 185 us
  between operations: 14.7 us -> 1.3 us
  matrix products: 4.71 us -> 0 us
    reduce_scatter x1 -> x0, waiting for transfers between devices: 219 us -> none  [per_device(): lax.psum_scatter(lax.dot_general(normed, query_grad, (((0,), (0,)), ((),...]
    pallas_call x1, Pallas kernels: 97.1 us -> 185 us  [run_chain(): pl.pallas_call(chain_kernel, out_shape=(jax.ShapeDtypeStruct((rows, width...]
    all_gather x1 -> x0, waiting for transfers between devices: 87.3 us -> none  [per_device(): weights = lax.all_gather(w_query[0], ('fsdp', 'seq'), axis=0, tiled=True)]
    dot_general x1 -> x0, matrix products: 4.71 us -> none  [per_device(): lax.dot_general(normed, query_grad, (((0,), (0,)), ((), ())), preferred_e...]
  transfers between devices with their start and end apart: 2 -> 0, of which waited for: 2 -> 0; matrix products, arithmetic and copies ran while one was open for 0% -> 0% of each run, Pallas kernels for 0% -> 0%
where the time goes in v2:
time: 189 us
  Pallas kernels  185 us (98%)
  local copies, waits for them, and re-layouts  2.47 us (1%)
    pallas_call x1, Pallas kernels, run_chain(): pl.pallas_call(chain_kernel, out_shape=(jax.ShapeDtypeStruct((rows, width...  185 us

profile of v2, /device:TPU:32, one launch (start us, length us, event | category | flops | bytes accessed | tf_op | source)
XLA Modules:
  0.0 189.2 jit_solution(1346287810928987198)
XLA Ops:
  1.3 185.5 %chain.1 = (bf16[128,1536]{1,0:T(8,128)(2,1)}, bf16[48,1536]{1,0:T(8,128)(2,1)}) custom-call(bf16[128,1536]{1,0:T(8,128)(2,1)} %bitcast.5, bf16[128,1536]{1,0:T(8,128)(2,1)} %bitcast.6, f32[1,1536]{1,0:T(1,128)} %gain_ref.1, f32[1,1536]{1,0:T(1,128)} %gate_ref.1, bf16[48,1536]{1,0:T(8,128)(2,1)} %bitcast.9, s32[1,8]{1,0:T(1,128)} %kept_ref.1, ...), custom_call_target="tpu_custom_call" | custom-call | tf_op jit(solution)/shard_map/chain/pallas_call | solution.py:455
  186.8 0.0 copy-start
  186.8 1.8 copy.12
  188.6 0.0 copy-done
  188.6 0.7 copy.13
Async XLA Ops:
  186.8 1.8 copy-start

commit v3 on v2

--- a/solution.py
+++ b/solution.py
@@ -18,8 +18,10 @@
 
 
 LINK_RATE = 85e3
-HOP_TIME = 1.7
-BLOCK_TIME = 0.6
+HOP_TIME = 1.9
+BLOCK_TIME = 0.5
+BACKLOG = 0.6
+LEFT_PARTS = 4
 
 
 def hops_of(size, flip):
@@ -42,7 +44,8 @@
                 before = len(plan) - 1
                 held.append((-sign * hop, before))
         for stream, (offset, source) in enumerate(held):
-            for sign, hops in hops_of(sizes[second], stream % 2 == 1):
+            flip = stream % 2 == 1 if second == 0 else stream % 4 != 0
+            for sign, hops in hops_of(sizes[second], flip):
                 before = source
                 for hop in range(1, hops + 1):
                     block = [0, 0]
@@ -95,26 +98,29 @@
     return plan, ends
 
 
-def run_plan(plan, part_bytes, ready):
+def run_plan(plan, part_bytes, ready, add_time=0.0):
+    cost = [part_bytes[message[3]] / LINK_RATE for message in plan]
+    tail = list(cost)
+    for index in reversed(range(len(plan))):
+        for dep in plan[index][4]:
+            tail[dep] = max(tail[dep], cost[dep] + HOP_TIME + tail[index])
+    order = sorted(range(len(plan)), key=lambda index: -tail[index])
     free, arrival, events = {}, {}, []
     done, started, now = set(), set(), 0.0
     made = set()
     todo = list(ready)
-
-    def launch():
-        for index, (axis, sign, block, part, deps) in enumerate(plan):
+    while len(done) < len(plan):
+        for index in order:
+            axis, sign, block, part, deps = plan[index]
             if index in started or any(dep not in done for dep in deps):
                 continue
-            if ready and block[0] not in made:
+            if (ready and block[0] not in made) or free.get((axis, sign), 0.0) > now + BACKLOG:
                 continue
             started.add(index)
-            begin = max(now, free.get((axis, sign), 0.0))
-            free[axis, sign] = begin + part_bytes[part] / LINK_RATE
+            now += add_time if deps else 0.0
+            free[axis, sign] = max(now, free.get((axis, sign), 0.0)) + cost[index]
             arrival[index] = free[axis, sign] + HOP_TIME
             events.append(("start", index))
-
-    launch()
-    while len(done) < len(plan):
         coming = sorted((when, index) for index, when in arrival.items() if index not in done)
         if todo and (not coming or coming[0][0] > now):
             step = todo.pop(0)
@@ -126,16 +132,21 @@
             now = max(now, when)
             done.add(index)
             events.append(("wait", index))
-        launch()
     return events
+
+
+def head_groups(heads):
+    sizes = [1] + [2] * ((heads - 2) // 2) + [1] if heads > 2 else [1] * heads
+    starts = [sum(sizes[:index]) for index in range(len(sizes))]
+    return [(start * HDIM, size * HDIM) for start, size in zip(starts, sizes)]
 
 
 def chain_kernel(
     x_ref, go_ref, gain_ref, gate_ref, shard_ref, kept_ref, links_ref,
     out_ref, grad_ref,
     w_ref, wgrad, slots_a, slots_b,
-    keys, inv_s, q_s, pt_s, kt_s, dy_buf, lr_send, lr_recv, kgo_s, ng_s, qg_s,
-    own_sem, turn, gsend, grecv, ssend, srecv,
+    keys, inv_s, mean_s, q_s, pt_s, kt_s, dy_buf, lr_send, lr_recv, kgo_s, ng_s, qg_s,
+    own_sem, gsend, grecv, ssend, srecv,
     nsend, nrecv, lsend, lrecv, dsend, drecv,
 ):
     sections = lax.axis_size("section")
@@ -145,14 +156,18 @@
     fsdp = lax.axis_index("fsdp")
     rows, width = x_ref.shape
     heads = width // HDIM
-    groups = width // GROUP
-    per_group = GROUP // HDIM
+    spans = head_groups(heads)
+    groups = len(spans)
     scale = HDIM ** (-0.5)
     ring_z = lax.axis_size("fsdp")
     shard = width // (ring_z * tiles)
     cut = first_columns(width)
     columns = (pl.ds(0, cut), pl.ds(cut, width - cut))
+    half = width // 256 * 128
+    gather_columns = (pl.ds(0, half), pl.ds(half, width - half))
     part_bytes = (2 * shard * cut, 2 * shard * (width - cut))
+    left_rows = rows // LEFT_PARTS
+    gather_bytes = (2 * shard * half, 2 * shard * (width - half), 2 * left_rows * width)
 
     def neighbour(axis, sign):
         if axis == 0:
@@ -184,7 +199,7 @@
         at = pl.ds(pl.multiple_of(step * 16, 16), 16)
         x_rows = x_ref[at, :].astype(jnp.float32)
         inv = lax.rsqrt(jnp.mean(x_rows * x_rows, axis=-1, keepdims=True) + norm_eps)
-        inv_s[at, :] = jnp.broadcast_to(inv, (16, 128))
+        inv_s[at, :] = jnp.broadcast_to(inv, (16, HDIM))
         rounded = (x_rows * inv * gain_ref[...]).astype(jnp.bfloat16)
         keys[pl.ds(pl.multiple_of(rows + step * 16, 16), 16), :] = rounded
         return carry
@@ -202,26 +217,20 @@
     pl.semaphore_wait(barrier, 6)
     own_copy.wait()
 
-    left_copy = pltpu.make_async_remote_copy(
-        src_ref=keys.at[pl.ds(rows, rows), :],
-        dst_ref=keys.at[pl.ds(0, rows), :],
-        send_sem=nsend,
-        recv_sem=nrecv,
-        device_id=(sec, fsdp, lax.rem(seq + 1, tiles)),
-        device_id_type=MESH,
-    )
-
-    @pl.when(seq < tiles - 1)
-    def _():
-        left_copy.start()
-
     gather = spread_plan(ring_z, tiles)
+    weight_count = len(gather)
+    gather = gather + [(1, 1, (0, 0), 2, [])] * (LEFT_PARTS if tiles > 1 else 0)
 
     def gather_copy(index):
         axis, sign, block, part, _ = gather[index]
-        place = w_ref.at[rows_of(block), columns[part]]
+        if part == 2:
+            step = (index - weight_count) * left_rows
+            source = keys.at[pl.ds(rows + step, left_rows), :]
+            place = keys.at[pl.ds(step, left_rows), :]
+        else:
+            source = place = w_ref.at[rows_of(block), gather_columns[part]]
         return pltpu.make_async_remote_copy(
-            src_ref=place,
+            src_ref=source,
             dst_ref=place,
             send_sem=gsend.at[index],
             recv_sem=grecv.at[index],
@@ -229,63 +238,47 @@
             device_id_type=MESH,
         )
 
-    if sections % 2 == 0:
-
-        @pl.when(lax.rem(sec, 2) == 0)
-        def _():
-            pl.semaphore_wait(turn, 1)
-
-    for kind, index in run_plan(gather, part_bytes, ()):
+    for kind, index in run_plan(gather, gather_bytes, ()):
+        left = gather[index][3] == 2
         if kind == "start":
-            gather_copy(index).start()
+            if left:
+
+                @pl.when(seq < tiles - 1)
+                def _():
+                    gather_copy(index).start()
+            else:
+                gather_copy(index).start()
+            continue
+        if left:
+
+            @pl.when(seq > 0)
+            def _():
+                gather_copy(index).wait_recv()
         else:
             gather_copy(index).wait_recv()
-    for index in range(len(gather)):
-        gather_copy(index).wait_send()
-    if sections % 2 == 0:
-
-        @pl.when(lax.rem(sec, 2) == 1)
-        def _():
-            pl.semaphore_signal(
-                turn, inc=1, device_id=(sec - 1, fsdp, seq), device_id_type=MESH
-            )
-
-    def query_block(step, carry):
-        at = pl.ds(pl.multiple_of(step * GROUP, GROUP), GROUP)
+
+    for start in range(0, width, GROUP):
+        at = pl.ds(start, GROUP)
         q_s[:, at] = mm(keys[rows:, :], w_ref[:, at]).astype(jnp.bfloat16)
-        return carry
-
-    lax.fori_loop(0, groups, query_block, 0)
-
-    @pl.when(seq > 0)
-    def _():
-        left_copy.wait_recv()
-
-    @pl.when(seq < tiles - 1)
-    def _():
-        left_copy.wait_send()
-
-    def probs_block(head, carry):
-        at = pl.ds(pl.multiple_of(head * HDIM, HDIM), HDIM)
+
+    position = lax.broadcasted_iota(jnp.int32, (2 * rows, rows), 0)
+    valid = position + linked * rows >= rows
+    for head in range(heads):
+        at = pl.ds(head * HDIM, HDIM)
         key_part = keys[:, at]
         scores = mm(key_part, q_s[:, at], NT) * scale
-        position = lax.broadcasted_iota(jnp.int32, scores.shape, 0)
-        valid = position + linked * rows >= rows
         scores = jnp.where(valid, scores, -1e30)
         top = jnp.max(scores, axis=0, keepdims=True)
         weight = jnp.exp(scores - top)
         pt_s[head] = weight / jnp.sum(weight, axis=0, keepdims=True)
         kt_s[at, :] = key_part.T
-        return carry
-
-    lax.fori_loop(0, heads, probs_block, 0)
 
     @pl.when(sec == sections - 1)
     def _():
         dy_buf[...] = go_ref[...]
 
     def dy_copy(group):
-        at = pl.ds(group * GROUP, GROUP)
+        at = pl.ds(*spans[group])
         return pltpu.make_async_remote_copy(
             src_ref=out_ref.at[:, at],
             dst_ref=dy_buf.at[:, at],
@@ -296,7 +289,7 @@
         )
 
     def lr_copy(group):
-        at = pl.ds(group * GROUP, GROUP)
+        at = pl.ds(*spans[group])
         return pltpu.make_async_remote_copy(
             src_ref=lr_send.at[:, at],
             dst_ref=lr_recv.at[:, at],
@@ -307,7 +300,8 @@
         )
 
     def attention(group):
-        for head in range(group * per_group, (group + 1) * per_group):
+        first, span = spans[group]
+        for head in range(first // HDIM, (first + span) // HDIM):
             at = pl.ds(head * HDIM, HDIM)
             grad = (gate_ref[:, at] * dy_buf[:, at].astype(jnp.float32)).astype(jnp.bfloat16)
             probs = pt_s[head]
@@ -323,7 +317,7 @@
             qg_s[:, at] = mm(kt_s[at, :], score_grad).astype(jnp.bfloat16).T
 
     def project(group):
-        at = pl.ds(group * GROUP, GROUP)
+        at = pl.ds(*spans[group])
         part = mm(qg_s[:, at], w_ref[:, at], NT)
         if group == 0:
             ng_s[...] = part
@@ -346,30 +340,55 @@
             project(group - 1)
     project(groups - 1)
 
-    @pl.when(seq < tiles - 1)
-    def _():
-        for group in range(groups):
-            lr_copy(group).wait_recv()
-
-    def finish_block(step, carry):
-        at = pl.ds(pl.multiple_of(step * 16, 16), 16)
-        x_rows = x_ref[at, :].astype(jnp.float32)
-        inv = inv_s[at, 0:1]
-        total = ng_s[at, :] + kgo_s[at, :] + lr_recv[at, :].astype(jnp.float32)
-        total = total * gain_ref[...]
-        mean_term = jnp.mean(x_rows * total, axis=-1, keepdims=True)
-        change = inv * (total - x_rows * (inv * inv * mean_term))
-        before = dy_buf[at, :].astype(jnp.float32)
-        kept_here = jnp.full(before.shape, keep, jnp.int32) > 0
-        out_ref[at, :] = jnp.where(kept_here, before + change, before).astype(jnp.bfloat16)
-        return carry
-
-    lax.fori_loop(0, rows // 16, finish_block, 0)
+    last = pl.ds(*spans[-1])
+    most = pl.ds(0, spans[-1][0])
+
+    def finish():
+        @pl.when(seq < tiles - 1)
+        def _():
+            for group in range(groups - 1):
+                lr_copy(group).wait_recv()
+
+        for start in range(0, rows, 16):
+            at = pl.ds(start, 16)
+            main = ng_s[at, most] + kgo_s[at, most] + lr_recv[at, most].astype(jnp.float32)
+            main = main * gain_ref[:, most]
+            ng_s[at, most] = main
+            rest = (ng_s[at, last] + kgo_s[at, last]) * gain_ref[:, last]
+            ng_s[at, last] = rest
+            mean = jnp.sum(x_ref[at, most].astype(jnp.float32) * main, axis=-1, keepdims=True)
+            mean = mean + jnp.sum(
+                x_ref[at, last].astype(jnp.float32) * rest, axis=-1, keepdims=True
+            )
+            mean_s[at, :] = jnp.broadcast_to(mean, (16, HDIM))
+
+        @pl.when(seq < tiles - 1)
+        def _():
+            lr_copy(groups - 1).wait_recv()
+
+        added = lr_recv[:, last].astype(jnp.float32) * gain_ref[:, last]
+        ng_s[:, last] += added
+        mean = jnp.sum(x_ref[:, last].astype(jnp.float32) * added, axis=-1, keepdims=True)
+        inv = inv_s[...]
+        mean_s[...] = (mean_s[...] + mean) * (inv * inv * (1.0 / width))
+        kept_here = jnp.full((rows, HDIM), keep, jnp.int32) > 0
+        for group, (first, span) in enumerate(spans):
+            for start in range(first, first + span, HDIM):
+                at = pl.ds(start, HDIM)
+                before = dy_buf[:, at].astype(jnp.float32)
+                x_part = x_ref[:, at].astype(jnp.float32)
+                change = inv_s[...] * (ng_s[:, at] - x_part * mean_s[...])
+                out_ref[:, at] = jnp.where(kept_here, before + change, before).astype(
+                    jnp.bfloat16
+                )
+
+            @pl.when(sec > 0)
+            def _():
+                dy_copy(group).start()
 
     @pl.when(sec > 0)
     def _():
-        for group in range(groups):
-            dy_copy(group).start()
+        finish()
 
     grads = qg_s[...].astype(jnp.float32)
     qg_s[...] = jnp.where(
@@ -405,23 +424,41 @@
         start = lax.rem(fsdp + offset + ring_z, ring_z) * span
         at = pl.ds(pl.multiple_of(start, shard), span)
         left = kt_s[at, rows : 2 * rows]
-        for group in range(groups):
-            to = pl.ds(group * GROUP, GROUP)
+        for first in range(0, width, GROUP):
+            to = pl.ds(first, GROUP)
             wgrad[at, to] = mm(left, qg_s[:, to]).astype(jnp.bfloat16)
 
     makes = []
     for offset in far_first(ring_z):
         makes.append((offset, offset - ring_z, offset + ring_z))
-    for kind, index in run_plan(sums, part_bytes, makes):
+    unmade = len(makes)
+    for kind, index in run_plan(sums, part_bytes, makes, 0.1):
         if kind == "make":
             make(index[0])
+            unmade -= 1
         elif kind == "start":
             _, _, block, part, adds = sums[index]
             if adds:
                 wgrad[rows_of(block), columns[part]] = summed(block, part, adds)
             sum_copy(index).start()
         else:
+            if unmade == 0:
+                unmade = -1
+
+                @pl.when(sec == 0)
+                def _():
+                    finish()
+
             sum_copy(index).wait_recv()
+    for index in range(len(gather)):
+        if gather[index][3] != 2:
+            gather_copy(index).wait_send()
+
+    @pl.when(seq < tiles - 1)
+    def _():
+        for index in range(weight_count, len(gather)):
+            gather_copy(index).wait_send()
+
     for part in (0, 1):
         grad_ref[:, columns[part]] = summed((0, 0), part, ends[part])
     for index in range(len(sums)):
@@ -445,7 +482,7 @@
 def run_chain(x, grad_out, gain, gate, shard, kept, links):
     rows, width = x.shape
     heads = width // HDIM
-    groups = width // GROUP
+    groups = len(head_groups(heads))
     vmem = pl.BlockSpec(memory_space=pltpu.VMEM)
     smem = pl.BlockSpec(memory_space=pltpu.SMEM)
     low = jnp.bfloat16
@@ -466,7 +503,8 @@
             pltpu.VMEM((count, shard.shape[0], cut), low),
             pltpu.VMEM((count, shard.shape[0], width - cut), low),
             pltpu.VMEM((2 * rows, width), low),
-            pltpu.VMEM((rows, 128), jnp.float32),
+            pltpu.VMEM((rows, HDIM), jnp.float32),
+            pltpu.VMEM((rows, HDIM), jnp.float32),
             pltpu.VMEM((rows, width), low),
             pltpu.VMEM((heads, 2 * rows, rows), jnp.float32),
             pltpu.VMEM((width, 2 * rows), low),
@@ -477,9 +515,8 @@
             pltpu.VMEM((rows, width), jnp.float32),
             pltpu.VMEM((rows, width), low),
             dma,
-            pltpu.SemaphoreType.REGULAR,
-            dma((2 * count,)),
-            dma((2 * count,)),
+            dma((2 * count + LEFT_PARTS,)),
+            dma((2 * count + LEFT_PARTS,)),
             dma((2 * count,)),
             dma((2 * count,)),
             dma,

time: 189 us -> 158 us (0.84)
  Pallas kernels: 185 us -> 153 us
    pallas_call x1, Pallas kernels: 185 us -> 153 us  [run_chain(): pl.pallas_call(chain_kernel, out_shape=(jax.ShapeDtypeStruct((rows, width...]
where the time goes in v3:
time: 158 us; the launch traced here: 157 us
  Pallas kernels  153 us (97%)
  local copies, waits for them, and re-layouts  2.47 us (2%)
    pallas_call x1, Pallas kernels, run_chain(): pl.pallas_call(chain_kernel, out_shape=(jax.ShapeDtypeStruct((rows, width...  153 us

profile of v3, /device:TPU:32, one launch (start us, length us, event | category | flops | bytes accessed | tf_op | source)
XLA Modules:
  0.0 157.1 jit_solution(2477439337953208020)
XLA Ops:
  1.3 153.4 %chain.1 = (bf16[128,1536]{1,0:T(8,128)(2,1)}, bf16[48,1536]{1,0:T(8,128)(2,1)}) custom-call(bf16[128,1536]{1,0:T(8,128)(2,1)} %bitcast.5, bf16[128,1536]{1,0:T(8,128)(2,1)} %bitcast.6, f32[1,1536]{1,0:T(1,128)} %gain_ref.1, f32[1,1536]{1,0:T(1,128)} %gate_ref.1, bf16[48,1536]{1,0:T(8,128)(2,1)} %bitcast.9, s32[1,8]{1,0:T(1,128)} %kept_ref.1, ...), custom_call_target="tpu_custom_call" | custom-call | tf_op jit(solution)/shard_map/chain/pallas_call | solution.py:492
  154.7 0.0 copy-start
  154.7 1.8 %copy.12 = bf16[1,1,128,1536]{3,2,1,0:T(8,128)(2,1)} copy(bf16[1,1,128,1536]{3,2,1,0:T(8,128)(2,1)} %bitcast.7) | data formatting | bytes 786432
  156.5 0.0 copy-done
  156.5 0.7 copy.13
Async XLA Ops:
  154.7 1.8 %copy-start = (bf16[48,1536]{1,0:T(8,128)(2,1)S(1)}, bf16[48,1536]{1,0:T(8,128)(2,1)}, u32[]{:S(2)}) copy-start(bf16[48,1536]{1,0:T(8,128)(2,1)} %get-tuple-element.5) | copy-start | bytes 442372
